TPU v7x, 256 devices: a whole 4x4x8 slice. The times are simulated.
256 devices in a mesh: dp: 16 (over z, core), mp: 16 (over y, x).
Axes of the slice: x: 4, y: 4, z: 8, core: 2. Of those that a mesh axis runs over, the one named last changes fastest.
Arguments:
- tokens: bfloat16 [49152, 8192], P('dp', 'mp'), may hold values from -6 to 6
- frozen_weight: bfloat16 [8192, 2048], P('mp', 'dp'), may hold values from -0.0625 to 0.0625
- adapter_down_weight: bfloat16 [8192, 4096], P(None, 'mp'), may hold values from -0.0625 to 0.0625
- adapter_up_weight: bfloat16 [2, 128, 16, 1024], P(None, 'mp'), may hold values from -1.5 to 1.5
- token_adapter_index: int32 [49152], P('dp'), may hold values from 0 to 127, as said below
Outputs:
- projected: bfloat16 [49152, 2048], P(('dp', 'mp'))
Inputs may be any that keep to these rules, and one draw needn't show every extreme that they name: `token_adapter_index`: A token's owner is its adapter id divided by 8, rounded down. Of the 192 tokens of each aligned block of rows (the rows of one device's output), at most 24 have the same owner; in each run of 16 such blocks that one dp index holds, one owner has exactly 24 tokens in every block.
All inputs are finite; a program needn't handle non-finite values.
Results may differ from a plain program's by a relative error of at most 0.0055.
Values may be sent and summed in bfloat16 or wider, within the bound.
A program may use at most 128 MiB of HBM per device.

v0:
```python
import jax
import jax.numpy as jnp
from jax import lax
from jax.sharding import PartitionSpec as P

ADAPTER_SCALE = 2.0


def local(tokens, frozen_weight, adapter_down_weight, adapter_up_weight, token_adapter_index):
    mp_count = lax.axis_size("mp")
    position = lax.axis_index("mp")
    group_rows, feature_cols = tokens.shape
    own_rows = group_rows // mp_count
    capacity = 2 * own_rows // mp_count
    hidden_width = adapter_down_weight.shape[0]
    present_adapters = adapter_up_weight.shape[1]
    rank_extent = adapter_up_weight.shape[2]
    key_value_span = adapter_up_weight.shape[3]
    both_width = 2 * key_value_span
    per_owner = mp_count * capacity
    slot_total = mp_count * per_owner
    owners_of = token_adapter_index // present_adapters
    local_adapter = token_adapter_index % present_adapters
    owner_hits = (owners_of[:, None] == jnp.arange(mp_count, dtype=jnp.int32)[None, :]).astype(
        jnp.int32
    )
    running = jnp.cumsum(owner_hits.reshape(mp_count, own_rows, mp_count), axis=1).reshape(
        group_rows, mp_count
    )
    order_in = jnp.sum(running * owner_hits, axis=1) - 1
    block_index = jnp.arange(group_rows, dtype=jnp.int32) // own_rows
    slot_index = owners_of * per_owner + block_index * capacity + order_in
    slot_token = (
        jnp.full((slot_total,), group_rows, jnp.int32)
        .at[slot_index]
        .set(jnp.arange(group_rows, dtype=jnp.int32))
    )
    slot_adapter = jnp.full((slot_total,), -1, jnp.int32).at[slot_index].set(local_adapter)
    padded = jnp.concatenate([tokens, jnp.zeros((1, feature_cols), tokens.dtype)], axis=0)
    outgoing = jnp.take(padded, slot_token, axis=0).reshape(
        mp_count, mp_count, capacity, feature_cols
    )
    labels = slot_adapter.reshape(mp_count, mp_count, capacity, 1)
    key_up_weight = adapter_up_weight[0].reshape(present_adapters * rank_extent, key_value_span)
    value_up_weight = adapter_up_weight[1].reshape(present_adapters * rank_extent, key_value_span)
    received = lax.all_to_all(outgoing, "mp", split_axis=0, concat_axis=3, tiled=True)
    tags = lax.all_to_all(labels, "mp", split_axis=0, concat_axis=3, tiled=True)
    items = received.shape[2]
    flat_tokens = received.reshape(-1, hidden_width)
    adapter_tag = tags[..., 0].reshape(-1)
    full_projection = jnp.dot(flat_tokens, adapter_down_weight, preferred_element_type=jnp.float32)
    selector = (
        adapter_tag[:, None] == jnp.arange(present_adapters, dtype=jnp.int32)[None, :]
    ).astype(jnp.float32)
    low_rows = (
        full_projection.reshape(-1, present_adapters, 2, rank_extent) * selector[:, :, None, None]
    ).astype(jnp.bfloat16)
    key_section = jnp.dot(
        low_rows[:, :, 0, :].reshape(-1, present_adapters * rank_extent),
        key_up_weight,
        preferred_element_type=jnp.float32,
    )
    value_section = jnp.dot(
        low_rows[:, :, 1, :].reshape(-1, present_adapters * rank_extent),
        value_up_weight,
        preferred_element_type=jnp.float32,
    )
    adapter_updates = (
        ADAPTER_SCALE * jnp.concatenate([key_section, value_section], axis=1)
    ).astype(jnp.bfloat16)
    adapter_updates = adapter_updates.reshape(1, mp_count, items, both_width)
    arrived = lax.all_to_all(adapter_updates, "mp", split_axis=1, concat_axis=0, tiled=True)
    weight_full = lax.all_gather(frozen_weight, "dp", axis=1, tiled=True)
    own_owner = lax.dynamic_slice_in_dim(owners_of, position * own_rows, own_rows)
    own_order = lax.dynamic_slice_in_dim(order_in, position * own_rows, own_rows)
    own_delta = arrived[own_owner, 0, own_order]
    base_rows = lax.psum_scatter(
        jnp.dot(tokens, weight_full, preferred_element_type=jnp.float32),
        "mp",
        scatter_dimension=0,
        tiled=True,
    )
    return (base_rows + own_delta.astype(jnp.float32)).astype(jnp.bfloat16)


def solution(mesh):
    placed = (P("dp", "mp"), P("mp", "dp"), P(None, "mp"), P(None, "mp", None, None), P("dp"))
    return jax.shard_map(
        local, mesh=mesh, in_specs=placed, out_specs=P(("dp", "mp"), None), check_vma=False
    )
```

profile of v0, /device:TPU:32, one launch (start us, length us, event | category | flops | bytes accessed | tf_op | source)
XLA Modules:
  0.0 337.2 jit_solution(10187303301574286426)
XLA Ops:
  6.5 0.0 all-gather.2.cloned.1.call-start
  6.5 0.7 all-gather.2.cloned.1.call-update
  7.3 0.0 reduce-scatter.2.cloned.1.call-start
  7.3 45.3 %all-gather.2.cloned.1.call-done = bf16[512,2048]{1,0:T(8,128)(2,1)} async-done(((bf16[512,128]{1,0:T(8,128)(2,1)}), bf16[512,2048]{1,0:T(8,128)(2,1)}) %all-gather.2.cloned.1.call-update) | async-done | bytes 2097168 | tf_op jit(solution)/shard_map/all_gather | solution.py:73
  52.6 13.7 %fusion.36 = f32[3072,2048]{1,0:T(8,128)} fusion(bf16[3072,512]{1,0:T(8,128)(2,1)} %param.5, bf16[512,2048]{1,0:T(8,128)(2,1)} %all-gather.2.cloned.1.call-done), kind=kOutput, calls=%fused_computation.67 | convolution fusion | flops 6442450944 | bytes 30408704 | tf_op jit(solution)/shard_map/dot_general | solution.py:78
  66.3 0.0 copy-start.1
  66.3 0.0 reduce-scatter.2.cloned.1.call-update
  66.3 0.7 copy-done.1
  67.0 0.1 eq.45
  67.2 9.1 %reduce-window.6 = s32[16,16,2,128]{3,1,2,0:T(8,128)S(1)} reduce-window(s32[16,16,2,128]{3,1,2,0:T(8,128)S(1)} %copy_bitcast_fusion, s32[]{:T(128)} %constant.65.clone.1), window={size=1x1x1x128 pad=0_0x0_0x0_0x127_0}, to_apply=%region_1.2 | reduce-window | flops 8323072 | bytes 524292 | tf_op jit(solution)/shard_map/reduce-window
  76.2 0.1 slice.37
  76.4 0.3 copy.22
  76.6 0.1 fusion.14
  76.7 0.1 bitcast_bitcast_fusion
  76.9 0.1 fusion.12
  77.0 0.1 sub.19
  77.1 11.8 %scatter_custom_fusion.1 = s32[6144]{0:T(1024)S(1)} fusion(s32[3072]{0:T(1024)S(1)} %get-tuple-element.10, s32[3072]{0:T(1024)S(1)} %get-tuple-element.9, s32[]{:T(128)} %constant.68.clone.1), kind=kCustom, calls=%fused_computation.46 | custom fusion | bytes 24580 | tf_op jit(solution)/shard_map/scatter | solution.py:38
  88.9 0.1 reshape.131
  89.0 0.7 reshape.188
  89.7 6.8 %all-to-all-start.1 = ((s32[16,1,384]{2,1,0:T(1,128)}), s32[16,1,384]{2,1,0:T(1,128)S(1)}, u32[]{:S(2)}, u32[]{:S(2)}) async-start(s32[16,1,384]{2,1,0:T(1,128)} %reshape.188), calls=%async_computation.2 | async-start | bytes 49152 | tf_op jit(solution)/shard_map/all_to_all | solution.py:47
  96.6 2.2 concatenate.20
  98.8 11.8 %scatter_custom_fusion = s32[6144]{0:T(1024)S(1)} fusion(s32[3072]{0:T(1024)S(1)} %get-tuple-element.10, s32[3072]{0:T(1024)S(1)} %iota.26, s32[]{:T(128)} %constant.63.clone.1), kind=kCustom, calls=%fused_computation.49 | custom fusion | bytes 24580 | tf_op jit(solution)/shard_map/scatter | solution.py:36
  110.6 0.1 broadcast_in_dim.40
  110.8 25.5 %gather_fusion = bf16[6144,512]{1,0:T(8,128)(2,1)} fusion(bf16[3073,512]{1,0:T(8,128)(2,1)S(1)} %concatenate.20, s32[6144]{0:T(1024)S(1)} %fusion.13), kind=kCustom, calls=%fused_computation | custom fusion | bytes 12607488 | tf_op jit(solution)/shard_map/jit(_take)/gather | solution.py:40
  136.3 6.9 %broadcast_select_fusion = bf16[16,16,24,512]{3,2,1,0:T(8,128)(2,1)} fusion(bf16[16,16,24,512]{3,2,1,0:T(8,128)(2,1)} %bitcast.74, pred[16,16,24]{2,1,0:T(8,128)(4,1)S(1)} %broadcast_in_dim.40), kind=kLoop, calls=%fused_computation.6 | loop fusion | flops 3145728 | bytes 12589056 | tf_op jit(solution)/shard_map/jit(_take)/select_n | solution.py:40
  143.1 0.0 all-to-all-done.1
  143.1 7.1 %all-to-all-start = ((bf16[16,16,24,512]{3,2,1,0:T(8,128)(2,1)}), bf16[16,16,24,512]{3,2,1,0:T(8,128)(2,1)}, u32[]{:S(2)}, u32[]{:S(2)}) async-start(bf16[16,16,24,512]{3,2,1,0:T(8,128)(2,1)} %broadcast_select_fusion), calls=%async_computation.1 | async-start | bytes 12582912 | tf_op jit(solution)/shard_map/all_to_all | solution.py:46
  150.3 0.0 copy-start
  150.3 6.6 %copy.26 = bf16[8192,256]{0,1:T(8,128)(2,1)} copy(bf16[8192,256]{1,0:T(8,128)(2,1)} %param.7) | data formatting | bytes 8388608 | tf_op args[2]
  156.9 0.0 copy-done
  156.9 0.5 broadcast.140
  157.5 0.7 reduce.1
  158.2 0.1 reshape.189
  158.3 0.1 eq.52
  158.4 107.1 %all-to-all-done = bf16[16,16,24,512]{3,2,1,0:T(8,128)(2,1)} async-done(((bf16[16,16,24,512]{3,2,1,0:T(8,128)(2,1)}), bf16[16,16,24,512]{3,2,1,0:T(8,128)(2,1)}, u32[]{:S(2)}, u32[]{:S(2)}) %all-to-all-start) | async-done | bytes 6291488 | tf_op jit(solution)/shard_map/all_to_all | solution.py:46
  265.5 10.0 %copy.25 = bf16[1,16,24,16,512]{4,3,2,1,0:T(8,128)(2,1)} copy(bf16[1,16,24,16,512]{4,2,1,3,0:T(8,128)(2,1)} %bitcast.4) | data formatting | bytes 12582912 | tf_op jit(solution)/shard_map/all_to_all | solution.py:46
  275.5 10.5 %reshape.180 = bf16[384,8192,1,1]{1,0,2,3:T(8,128)(2,1)} reshape(bf16[1,16,24,16,512]{4,3,2,1,0:T(8,128)(2,1)} %copy.25) | data formatting | bytes 12582912 | tf_op jit(solution)/shard_map/reshape | solution.py:49
  286.0 6.5 %fusion.7 = bf16[384,8,2,16]{0,3,2,1:T(8,128)(2,1)S(1)} fusion(bf16[8,2,16,8192]{3,2,1,0:T(8,128)(2,1)} %bitcast.75, bf16[384,8192,1,1]{1,0,2,3:T(8,128)(2,1)} %reshape.180, f32[384,8]{0,1:T(8,128)S(1)} %fusion.26), kind=kOutput, calls=%fused_computation.14 | convolution fusion | flops 1610809344 | bytes 10694656 | tf_op jit(solution)/shard_map/dot_general | solution.py:51
  292.6 0.7 reshape.133
  293.2 0.7 reshape.132
  293.9 0.4 convolution_bitcast_fusion
  294.3 0.4 convolution_bitcast_fusion.1
  294.8 1.5 fusion.3
  296.2 3.9 %all-to-all-start.2 = ((bf16[1,16,24,2048]{3,2,0,1:T(8,128)(2,1)}), bf16[1,16,24,2048]{3,2,0,1:T(8,128)(2,1)S(1)}, u32[]{:S(2)}, u32[]{:S(2)}) async-start(bf16[1,16,24,2048]{3,2,0,1:T(8,128)(2,1)} %fusion.3), calls=%async_computation.3 | async-start | bytes 3145728 | tf_op jit(solution)/shard_map/all_to_all | solution.py:72
  300.2 0.1 fusion.31
  300.3 22.9 %all-to-all-done.2 = bf16[1,16,24,2048]{3,2,0,1:T(8,128)(2,1)S(1)} async-done(((bf16[1,16,24,2048]{3,2,0,1:T(8,128)(2,1)}), bf16[1,16,24,2048]{3,2,0,1:T(8,128)(2,1)S(1)}, u32[]{:S(2)}, u32[]{:S(2)}) %all-to-all-start.2) | async-done | bytes 1572896 | tf_op jit(solution)/shard_map/all_to_all | solution.py:72
  323.2 4.7 %gather_fusion.1 = bf16[192,2048]{1,0:T(8,128)(2,1)S(1)} fusion(bf16[16,1,24,2048]{3,2,1,0:T(8,128)(2,1)S(1)} %bitcast.73, s32[192]{0:T(256)S(1)} %fusion.31), kind=kCustom, calls=%fused_computation.1 | custom fusion | bytes 1575168 | tf_op jit(solution)/shard_map/gather | solution.py:76
  327.8 0.0 reduce-scatter.2.cloned.1.call-done
  327.9 2.5 add_convert_fusion
  (16 shorter events, 0.2 us)
Async XLA Ops:
  6.5 46.0 %all-gather.2.cloned.1.call-start = ((), (), s32[]{:S(2)}) async-start(), calls=%async_computation.4 | async-start | bytes 2228224 | tf_op jit(solution)/shard_map/all_gather | solution.py:73
  7.3 320.6 %reduce-scatter.2.cloned.1.call-start = ((), (), s32[]{:S(2)}) async-start(), calls=%async_computation.5 | async-start | bytes 26738688 | tf_op jit(solution)/shard_map/reduce_scatter | solution.py:77
  66.3 0.7 copy-start.1
  89.7 53.4 %all-to-all-start.1 = ((s32[16,1,384]{2,1,0:T(1,128)}), s32[16,1,384]{2,1,0:T(1,128)S(1)}, u32[]{:S(2)}, u32[]{:S(2)}) async-start(s32[16,1,384]{2,1,0:T(1,128)} %reshape.188), calls=%async_computation.2 | async-start | bytes 49152 | tf_op jit(solution)/shard_map/all_to_all | solution.py:47
  143.1 122.3 %all-to-all-start = ((bf16[16,16,24,512]{3,2,1,0:T(8,128)(2,1)}), bf16[16,16,24,512]{3,2,1,0:T(8,128)(2,1)}, u32[]{:S(2)}, u32[]{:S(2)}) async-start(bf16[16,16,24,512]{3,2,1,0:T(8,128)(2,1)} %broadcast_select_fusion), calls=%async_computation.1 | async-start | bytes 12582912 | tf_op jit(solution)/shard_map/all_to_all | solution.py:46
  150.3 6.6 %copy-start = (bf16[2,8,16,1024]{3,2,1,0:T(8,128)(2,1)S(1)}, bf16[2,8,16,1024]{3,2,1,0:T(8,128)(2,1)}, u32[]{:S(2)}) copy-start(bf16[2,8,16,1024]{3,2,1,0:T(8,128)(2,1)} %param.8) | copy-start | bytes 1572868
  296.2 26.9 %all-to-all-start.2 = ((bf16[1,16,24,2048]{3,2,0,1:T(8,128)(2,1)}), bf16[1,16,24,2048]{3,2,0,1:T(8,128)(2,1)S(1)}, u32[]{:S(2)}, u32[]{:S(2)}) async-start(bf16[1,16,24,2048]{3,2,0,1:T(8,128)(2,1)} %fusion.3), calls=%async_computation.3 | async-start | bytes 3145728 | tf_op jit(solution)/shard_map/all_to_all | solution.py:72
Sparse Core Ops, SparseCore 0:
  9.1 43.4 all-gather.1
  66.4 230.8 reduce-scatter.1
where the time goes:
time: 338 us; the launch traced here: 337 us
  waiting for transfers between devices  176 us (52%)
  local copies, waits for them, and re-layouts  87.4 us (26%)
  other arithmetic  21.1 us (6%)
  matrix products  21 us (6%)
  starting transfers between devices  17.9 us (5%)
  between operations  13.7 us (4%)
    all_to_all x1, waiting for transfers between devices, local(): lax.all_to_all(outgoing, 'mp', split_axis=0, concat_axis=3, tiled=True)  107 us
    all_gather x1, waiting for transfers between devices, local(): weight_full = lax.all_gather(frozen_weight, 'dp', axis=1, tiled=True)  45.3 us
    gather x1, local copies, waits for them, and re-layouts, local(): jnp.take(padded, slot_token, axis=0)  25.5 us
    all_to_all x1, waiting for transfers between devices, local(): lax.all_to_all(adapter_updates, 'mp', split_axis=1, concat_axis=0, tiled=...  22.9 us
    dot_general x1, matrix products, local(): jnp.dot(tokens, weight_full, preferred_element_type=jnp.float32)  13.7 us
    scatter x1, local copies, waits for them, and re-layouts, local(): jnp.full((slot_total,), -1, jnp.int32).at[slot_index].set(local_adapter)  11.8 us
    scatter x1, local copies, waits for them, and re-layouts, local(): slot_token = jnp.full((slot_total,), group_rows, jnp.int32).at[slot_index...  11.8 us
    reshape x1, local copies, waits for them, and re-layouts, local(): flat_tokens = received.reshape(-1, hidden_width)  10.5 us
  transfers between devices with their start and end apart: 5, of which 3 were waited for; matrix products, arithmetic and copies ran while one was open for 33% of the time, Pallas kernels for 0%

commit v1 on v0

--- a/solution.py
+++ b/solution.py
@@ -1,9 +1,20 @@
+import functools
 import jax
 import jax.numpy as jnp
 from jax import lax
 from jax.sharding import PartitionSpec as P
 
 ADAPTER_SCALE = 2.0
+
+
+def widths_pack(arr, dim_at):
+    rack = []
+    for _ in range(lax.axis_size("dp")):
+        rack.append(arr)
+    return jnp.concatenate(lax.all_to_all(jnp.stack(rack), "dp", 0, 0), dim_at)
+
+
+shape_goods_now = functools.partial(widths_pack, dim_at=1)
 
 
 def local(tokens, frozen_weight, adapter_down_weight, adapter_up_weight, token_adapter_index):
@@ -70,7 +81,7 @@
     ).astype(jnp.bfloat16)
     adapter_updates = adapter_updates.reshape(1, mp_count, items, both_width)
     arrived = lax.all_to_all(adapter_updates, "mp", split_axis=1, concat_axis=0, tiled=True)
-    weight_full = lax.all_gather(frozen_weight, "dp", axis=1, tiled=True)
+    weight_full = shape_goods_now(frozen_weight)
     own_owner = lax.dynamic_slice_in_dim(owners_of, position * own_rows, own_rows)
     own_order = lax.dynamic_slice_in_dim(order_in, position * own_rows, own_rows)
     own_delta = arrived[own_owner, 0, own_order]

time: 338 us -> 354 us (1.047); the launches traced: 337 us -> 348 us
  blocking collectives: 0 us -> 56.6 us
  waiting for transfers between devices: 176 us -> 131 us
    all_to_all x0 -> x1, blocking collectives: none -> 56.6 us  [widths_pack(): return jnp.concatenate(lax.all_to_all(jnp.stack(rack), 'dp', 0, 0), dim_at)]
    all_gather x1 -> x0, waiting for transfers between devices: 45.3 us -> none  [local(): weight_full = lax.all_gather(frozen_weight, 'dp', axis=1, tiled=True)]
    unnamed x8 -> x11, local copies, waits for them, and re-layouts: 8.14 us -> 9.22 us
  transfers between devices with their start and end apart: 5 -> 4, of which waited for: 3 -> 2; matrix products, arithmetic and copies ran while one was open for 33% -> 32% of each run, Pallas kernels for 0% -> 0%
where the time goes in v1:
time: 354 us; the launch traced here: 348 us
  waiting for transfers between devices  131 us (37%)
  local copies, waits for them, and re-layouts  88.1 us (25%)
  blocking collectives  56.6 us (16%)
  other arithmetic  21.1 us (6%)
  matrix products  19.2 us (5%)
  starting transfers between devices  18.2 us (5%)
  between operations  13.7 us (4%)
    all_to_all x1, waiting for transfers between devices, local(): lax.all_to_all(outgoing, 'mp', split_axis=0, concat_axis=3, tiled=True)  107 us
    all_to_all x1, blocking collectives, widths_pack(): return jnp.concatenate(lax.all_to_all(jnp.stack(rack), 'dp', 0, 0), dim_at)  56.6 us
    gather x1, local copies, waits for them, and re-layouts, local(): jnp.take(padded, slot_token, axis=0)  25.5 us
    all_to_all x1, waiting for transfers between devices, local(): lax.all_to_all(adapter_updates, 'mp', split_axis=1, concat_axis=0, tiled=...  23.5 us
    dot_general x1, matrix products, local(): jnp.dot(tokens, weight_full, preferred_element_type=jnp.float32)  11.9 us
    scatter x1, local copies, waits for them, and re-layouts, local(): jnp.full((slot_total,), -1, jnp.int32).at[slot_index].set(local_adapter)  11.8 us
    scatter x1, local copies, waits for them, and re-layouts, local(): slot_token = jnp.full((slot_total,), group_rows, jnp.int32).at[slot_index...  11.8 us
    reshape x1, local copies, waits for them, and re-layouts, local(): flat_tokens = received.reshape(-1, hidden_width)  10.5 us
  transfers between devices with their start and end apart: 4, of which 2 were waited for; matrix products, arithmetic and copies ran while one was open for 32% of the time, Pallas kernels for 0%

profile of v1, /device:TPU:32, one launch (start us, length us, event | category | flops | bytes accessed | tf_op | source)
XLA Modules:
  0.0 347.7 jit_solution(13641599443898458680)
XLA Ops:
  6.5 0.0 reduce-scatter.2.cloned.1.call-start
  6.5 1.0 copy.22
  7.5 0.0 copy-start
  7.6 0.2 stack.2
  7.8 56.6 %all_to_all.50 = bf16[16,512,128]{1,2,0:T(8,128)(2,1)S(1)} all-to-all(bf16[16,512,128]{1,2,0:T(8,128)(2,1)S(1)} %stack.2), channel_id=1, replica_groups=mesh['dp'=16,'mp'=16] {'dp'}, dimensions={0} | all-to-all | bytes 4194304 | tf_op jit(solution)/shard_map/all_to_all | solution.py:14
  64.3 0.0 copy-done
  64.3 11.9 %fusion.36 = f32[3072,2048]{1,0:T(8,128)} fusion(bf16[3072,512]{1,0:T(8,128)(2,1)S(1)} %copy-done, bf16[512,2048]{0,1:T(8,128)(2,1)S(1)} %bitcast.79), kind=kOutput, calls=%fused_computation.67 | convolution fusion | flops 6442450944 | bytes 30408704 | tf_op jit(solution)/shard_map/dot_general | solution.py:89
  76.3 0.0 copy-start.2
  76.3 0.0 reduce-scatter.2.cloned.1.call-update
  76.3 0.7 copy-done.2
  77.0 0.1 eq.45
  77.1 9.1 %reduce-window.6 = s32[16,16,2,128]{3,1,2,0:T(8,128)S(1)} reduce-window(s32[16,16,2,128]{3,1,2,0:T(8,128)S(1)} %copy_bitcast_fusion, s32[]{:T(128)} %constant.65.clone.1), window={size=1x1x1x128 pad=0_0x0_0x0_0x127_0}, to_apply=%region_1.2 | reduce-window | flops 8323072 | bytes 524292 | tf_op jit(solution)/shard_map/reduce-window
  86.2 0.1 slice.37
  86.4 0.3 copy.24
  86.6 0.1 fusion.14
  86.7 0.1 bitcast_bitcast_fusion
  86.8 0.1 fusion.12
  86.9 0.1 sub.19
  87.0 11.8 %scatter_custom_fusion.1 = s32[6144]{0:T(1024)S(1)} fusion(s32[3072]{0:T(1024)S(1)} %get-tuple-element.10, s32[3072]{0:T(1024)S(1)} %get-tuple-element.9, s32[]{:T(128)} %constant.68.clone.1), kind=kCustom, calls=%fused_computation.46 | custom fusion | bytes 24580 | tf_op jit(solution)/shard_map/scatter | solution.py:49
  98.8 0.1 reshape.141
  99.0 0.7 reshape.198
  99.7 7.0 %all-to-all-start.2 = ((s32[16,1,384]{2,1,0:T(1,128)}), s32[16,1,384]{2,1,0:T(1,128)S(1)}, u32[]{:S(2)}, u32[]{:S(2)}) async-start(s32[16,1,384]{2,1,0:T(1,128)} %reshape.198), calls=%async_computation.3 | async-start | bytes 49152 | tf_op jit(solution)/shard_map/all_to_all | solution.py:58
  106.8 2.2 concatenate.20
  109.0 11.8 %scatter_custom_fusion = s32[6144]{0:T(1024)S(1)} fusion(s32[3072]{0:T(1024)S(1)} %get-tuple-element.10, s32[3072]{0:T(1024)S(1)} %iota.26, s32[]{:T(128)} %constant.63.clone.1), kind=kCustom, calls=%fused_computation.49 | custom fusion | bytes 24580 | tf_op jit(solution)/shard_map/scatter | solution.py:47
  120.8 0.1 broadcast_in_dim.40
  120.9 25.5 %gather_fusion = bf16[6144,512]{1,0:T(8,128)(2,1)} fusion(bf16[3073,512]{1,0:T(8,128)(2,1)S(1)} %concatenate.20, s32[6144]{0:T(1024)S(1)} %fusion.13), kind=kCustom, calls=%fused_computation | custom fusion | bytes 12607488 | tf_op jit(solution)/shard_map/jit(_take)/gather | solution.py:51
  146.4 6.9 %broadcast_select_fusion = bf16[16,16,24,512]{3,2,1,0:T(8,128)(2,1)} fusion(bf16[16,16,24,512]{3,2,1,0:T(8,128)(2,1)} %bitcast.77, pred[16,16,24]{2,1,0:T(8,128)(4,1)S(1)} %broadcast_in_dim.40), kind=kLoop, calls=%fused_computation.6 | loop fusion | flops 3145728 | bytes 12589056 | tf_op jit(solution)/shard_map/jit(_take)/select_n | solution.py:51
  153.3 0.0 all-to-all-done.2
  153.3 7.2 %all-to-all-start.1 = ((bf16[16,16,24,512]{3,2,1,0:T(8,128)(2,1)}), bf16[16,16,24,512]{3,2,1,0:T(8,128)(2,1)}, u32[]{:S(2)}, u32[]{:S(2)}) async-start(bf16[16,16,24,512]{3,2,1,0:T(8,128)(2,1)} %broadcast_select_fusion), calls=%async_computation.2 | async-start | bytes 12582912 | tf_op jit(solution)/shard_map/all_to_all | solution.py:57
  160.5 0.0 copy-start.1
  160.5 6.7 %copy.28 = bf16[8192,256]{0,1:T(8,128)(2,1)} copy(bf16[8192,256]{1,0:T(8,128)(2,1)} %param.7) | data formatting | bytes 8388608 | tf_op args[2]
  167.2 0.0 copy-done.1
  167.3 0.5 broadcast.142
  167.8 0.7 reduce.1
  168.5 0.1 reshape.199
  168.6 0.1 eq.52
  168.7 107.3 %all-to-all-done.1 = bf16[16,16,24,512]{3,2,1,0:T(8,128)(2,1)} async-done(((bf16[16,16,24,512]{3,2,1,0:T(8,128)(2,1)}), bf16[16,16,24,512]{3,2,1,0:T(8,128)(2,1)}, u32[]{:S(2)}, u32[]{:S(2)}) %all-to-all-start.1) | async-done | bytes 6291488 | tf_op jit(solution)/shard_map/all_to_all | solution.py:57
  276.0 9.5 %copy.27 = bf16[1,16,24,16,512]{4,3,2,1,0:T(8,128)(2,1)} copy(bf16[1,16,24,16,512]{4,2,1,3,0:T(8,128)(2,1)} %bitcast.6) | data formatting | bytes 12582912 | tf_op jit(solution)/shard_map/all_to_all | solution.py:57
  285.5 10.5 %reshape.190 = bf16[384,8192,1,1]{1,0,2,3:T(8,128)(2,1)} reshape(bf16[1,16,24,16,512]{4,3,2,1,0:T(8,128)(2,1)} %copy.27) | data formatting | bytes 12582912 | tf_op jit(solution)/shard_map/reshape | solution.py:60
  296.0 6.5 %fusion.7 = bf16[384,8,2,16]{0,3,2,1:T(8,128)(2,1)S(1)} fusion(bf16[8,2,16,8192]{3,2,1,0:T(8,128)(2,1)} %bitcast.78, bf16[384,8192,1,1]{1,0,2,3:T(8,128)(2,1)} %reshape.190, f32[384,8]{0,1:T(8,128)S(1)} %fusion.26), kind=kOutput, calls=%fused_computation.14 | convolution fusion | flops 1610809344 | bytes 10694656 | tf_op jit(solution)/shard_map/dot_general | solution.py:62
  302.5 0.7 reshape.143
  303.2 0.7 reshape.142
  303.9 0.4 convolution_bitcast_fusion
  304.3 0.4 convolution_bitcast_fusion.1
  304.7 1.5 fusion.3
  306.2 3.9 %all-to-all-start.3 = ((bf16[1,16,24,2048]{3,2,0,1:T(8,128)(2,1)}), bf16[1,16,24,2048]{3,2,0,1:T(8,128)(2,1)S(1)}, u32[]{:S(2)}, u32[]{:S(2)}) async-start(bf16[1,16,24,2048]{3,2,0,1:T(8,128)(2,1)} %fusion.3), calls=%async_computation.4 | async-start | bytes 3145728 | tf_op jit(solution)/shard_map/all_to_all | solution.py:83
  310.1 0.1 fusion.31
  310.2 23.5 %all-to-all-done.3 = bf16[1,16,24,2048]{3,2,0,1:T(8,128)(2,1)S(1)} async-done(((bf16[1,16,24,2048]{3,2,0,1:T(8,128)(2,1)}), bf16[1,16,24,2048]{3,2,0,1:T(8,128)(2,1)S(1)}, u32[]{:S(2)}, u32[]{:S(2)}) %all-to-all-start.3) | async-done | bytes 1572896 | tf_op jit(solution)/shard_map/all_to_all | solution.py:83
  333.7 4.7 %gather_fusion.1 = bf16[192,2048]{1,0:T(8,128)(2,1)S(1)} fusion(bf16[16,1,24,2048]{3,2,1,0:T(8,128)(2,1)S(1)} %bitcast.76, s32[192]{0:T(256)S(1)} %fusion.31), kind=kCustom, calls=%fused_computation.1 | custom fusion | bytes 1575168 | tf_op jit(solution)/shard_map/gather | solution.py:87
  338.3 0.0 reduce-scatter.2.cloned.1.call-done
  338.4 2.5 add_convert_fusion
  (16 shorter events, 0.2 us)
Async XLA Ops:
  6.5 331.8 %reduce-scatter.2.cloned.1.call-start = ((), (), s32[]{:S(2)}) async-start(), calls=%async_computation.5 | async-start | bytes 26738688 | tf_op jit(solution)/shard_map/reduce_scatter | solution.py:88
  7.5 56.8 %copy-start = (bf16[3072,512]{1,0:T(8,128)(2,1)S(1)}, bf16[3072,512]{1,0:T(8,128)(2,1)}, u32[]{:S(2)}) copy-start(bf16[3072,512]{1,0:T(8,128)(2,1)} %param.5) | copy-start | bytes 9437188
  76.3 0.7 copy-start.2
  99.7 53.6 %all-to-all-start.2 = ((s32[16,1,384]{2,1,0:T(1,128)}), s32[16,1,384]{2,1,0:T(1,128)S(1)}, u32[]{:S(2)}, u32[]{:S(2)}) async-start(s32[16,1,384]{2,1,0:T(1,128)} %reshape.198), calls=%async_computation.3 | async-start | bytes 49152 | tf_op jit(solution)/shard_map/all_to_all | solution.py:58
  153.3 122.7 %all-to-all-start.1 = ((bf16[16,16,24,512]{3,2,1,0:T(8,128)(2,1)}), bf16[16,16,24,512]{3,2,1,0:T(8,128)(2,1)}, u32[]{:S(2)}, u32[]{:S(2)}) async-start(bf16[16,16,24,512]{3,2,1,0:T(8,128)(2,1)} %broadcast_select_fusion), calls=%async_computation.2 | async-start | bytes 12582912 | tf_op jit(solution)/shard_map/all_to_all | solution.py:57
  160.5 6.7 %copy-start.1 = (bf16[2,8,16,1024]{3,2,1,0:T(8,128)(2,1)S(1)}, bf16[2,8,16,1024]{3,2,1,0:T(8,128)(2,1)}, u32[]{:S(2)}) copy-start(bf16[2,8,16,1024]{3,2,1,0:T(8,128)(2,1)} %param.8) | copy-start | bytes 1572868
  306.2 27.5 %all-to-all-start.3 = ((bf16[1,16,24,2048]{3,2,0,1:T(8,128)(2,1)}), bf16[1,16,24,2048]{3,2,0,1:T(8,128)(2,1)S(1)}, u32[]{:S(2)}, u32[]{:S(2)}) async-start(bf16[1,16,24,2048]{3,2,0,1:T(8,128)(2,1)} %fusion.3), calls=%async_computation.4 | async-start | bytes 3145728 | tf_op jit(solution)/shard_map/all_to_all | solution.py:83
Sparse Core Ops, SparseCore 0:
  76.4 231.8 reduce-scatter.1
